TPU v7x, 256 devices: a whole 4x4x8 slice. The times are simulated.
256 devices in a mesh: row: 8 (over x, core), col: 16 (over z, y_hi), layer: 2 (over y_lo).
Axes of the slice: x: 4, y: 4 (y_hi: 2, y_lo: 2; y = y_hi * 2 + y_lo), z: 8, core: 2. Of those that a mesh axis runs over, the one named last changes fastest.
Arguments:
- interface_panel: float32 [2048, 1024], P('col', 'row'), may hold values from -6 to 6
- coupling: float32 [2, 2, 2048, 2048], P('layer', None, 'row', 'col'), may hold values from -0.0625 to 0.0625
- solved_coupling: float32 [8192, 1024], P(('layer', 'col'), 'row'), may hold values from -6 to 6
Outputs:
- schur_panel: float32 [2048, 1024], P('col', 'row')
All inputs are finite; a program needn't handle non-finite values.
Results may differ from a plain program's by a relative error of at most 0.00007.
Values sent between devices are 32-bit elements; how exact they have to be, the bound alone decides.
A program may use at most 64 MiB of HBM per device.

v0:
```python
import jax
import jax.numpy as jnp
from jax import lax
from jax.sharding import PartitionSpec as P


def shards(interface_panel, coupling, solved_coupling):
    blocks = coupling[0]
    depth = blocks.shape[0] * blocks.shape[1] * lax.axis_size("row")
    gathered_b = lax.all_gather(blocks, "row", axis=1, tiled=True).reshape(depth, blocks.shape[2])
    gathered_y = lax.all_gather(solved_coupling, "col", axis=0, tiled=True)
    partial = lax.dot_general(
        gathered_b,
        gathered_y,
        (((0,), (0,)), ((), ())),
        precision=lax.Precision.HIGHEST,
        preferred_element_type=jnp.float32,
    )
    other = lax.ppermute(partial, "layer", [(0, 1), (1, 0)])
    return interface_panel - (partial + other)


def solution(mesh):
    return jax.shard_map(
        shards,
        mesh=mesh,
        in_specs=(P("col", "row"), P("layer", None, "row", "col"), P(("layer", "col"), "row")),
        out_specs=P("col", "row"),
        check_vma=False,
    )
```

profile of v0, /device:TPU:2, one launch (start us, length us, event | category | flops | bytes accessed | tf_op | source)
XLA Modules:
  0.0 145.9 jit_solution(16994233739036828383)
XLA Ops:
  6.5 0.0 all-gather.6.cloned.1.call-start
  6.5 0.7 all-gather.6.cloned.1.call-update
  7.3 0.0 all-gather.4.cloned.1.call-start
  7.3 0.7 all-gather.4.cloned.1.call-update
  8.0 31.0 %all-gather.6.cloned.1.call-done = f32[1,2,2048,128]{3,2,1,0:T(8,128)} async-done(((f32[1,2,256,128]{3,2,1,0:T(8,128)}), f32[1,2,2048,128]{3,2,1,0:T(8,128)}) %all-gather.6.cloned.1.call-update) | async-done | bytes 2097168 | tf_op jit(solution)/shard_map/all_gather | solution.py:10
  39.0 89.4 %all-gather.4.cloned.1.call-done = f32[4096,128]{1,0:T(8,128)} async-done(((f32[256,128]{1,0:T(8,128)}), f32[4096,128]{1,0:T(8,128)}) %all-gather.4.cloned.1.call-update) | async-done | bytes 2097168 | tf_op jit(solution)/shard_map/all_gather | solution.py:11
  128.4 0.0 copy-start
  128.4 5.7 %fusion = f32[128,128]{1,0:T(8,128)S(1)} fusion(f32[4096,128]{1,0:T(8,128)} %bitcast.3, f32[4096,128]{1,0:T(8,128)} %all-gather.4.cloned.1.call-done), kind=kOutput, calls=%fused_computation.1 | convolution fusion | flops 805306368 | bytes 4259840 | tf_op jit(solution)/shard_map/dot_general | solution.py:12
  134.1 0.7 collective-permute-start
  134.7 3.7 %collective-permute-done = f32[128,128]{1,0:T(8,128)S(1)} collective-permute-done((f32[128,128]{1,0:T(8,128)S(1)}, f32[128,128]{1,0:T(8,128)S(1)}, u32[]{:S(2)}, u32[]{:S(2)}) %collective-permute-start) | collective-permute-done | bytes 65568 | tf_op jit(solution)/shard_map/ppermute | solution.py:19
  138.4 0.0 copy-done
  138.4 0.6 add_subtract_fusion
Async XLA Ops:
  6.5 32.4 %all-gather.6.cloned.1.call-start = ((), (), s32[]{:S(2)}) async-start(), calls=%async_computation.1 | async-start | bytes 2359296 | tf_op jit(solution)/shard_map/all_gather | solution.py:10
  7.3 121.1 %all-gather.4.cloned.1.call-start = ((), (), s32[]{:S(2)}) async-start(), calls=%async_computation | async-start | bytes 2228224 | tf_op jit(solution)/shard_map/all_gather | solution.py:11
  128.4 10.1 %copy-start = (f32[128,128]{1,0:T(8,128)S(1)}, f32[128,128]{1,0:T(8,128)}, u32[]{:S(2)}) copy-start(f32[128,128]{1,0:T(8,128)} %param.3) | copy-start | bytes 196612
  134.1 4.4 %collective-permute-start = (f32[128,128]{1,0:T(8,128)S(1)}, f32[128,128]{1,0:T(8,128)S(1)}, u32[]{:S(2)}, u32[]{:S(2)}) collective-permute-start(f32[128,128]{1,0:T(8,128)S(1)} %fusion), channel_id=1, source_target_pairs={{0,1},{1,0},{2,3},{3,2},{4,5},{5,4},{6,7},{7,6},{8,9},{9,8},{10,11... | collective-permute-start | bytes 196616 | tf_op jit(solution)/shard_map/ppermute | solution.py:19
Sparse Core Ops, SparseCore 0:
  9.2 29.7 all-gather.5
  41.6 86.7 all-gather.3
where the time goes:
time: 146 us
  waiting for transfers between devices  125 us (86%)
  between operations  13.4 us (9%)
  matrix products  5.7 us (4%)
    all_gather x1, waiting for transfers between devices, shards(): gathered_y = lax.all_gather(solved_coupling, 'col', axis=0, tiled=True)  89.4 us
    all_gather x1, waiting for transfers between devices, shards(): lax.all_gather(blocks, 'row', axis=1, tiled=True)  31 us
    dot_general x1, matrix products, shards(): lax.dot_general(gathered_b, gathered_y, (((0,), (0,)), ((), ())), precisi...  5.7 us
    ppermute x1, waiting for transfers between devices, shards(): other = lax.ppermute(partial, 'layer', [(0, 1), (1, 0)])  3.68 us
  transfers between devices with their start and end apart: 3, of which 3 were waited for; matrix products, arithmetic and copies ran while one was open for 0% of the time, Pallas kernels for 0%

commit v1 on v0

--- a/solution.py
+++ b/solution.py
@@ -5,9 +5,16 @@
 
 
 def shards(interface_panel, coupling, solved_coupling):
+
+    def pass_figure_on(w_in):
+        q_n = lax.axis_size("row")
+        tray = [q_n if hop_no == 1 else 1 for hop_no in range(w_in.ndim)]
+        carry = lax.all_to_all(jnp.tile(w_in, tray), "row", split_axis=1, concat_axis=1, tiled=True)
+        return carry
+
     blocks = coupling[0]
     depth = blocks.shape[0] * blocks.shape[1] * lax.axis_size("row")
-    gathered_b = lax.all_gather(blocks, "row", axis=1, tiled=True).reshape(depth, blocks.shape[2])
+    gathered_b = pass_figure_on(blocks).reshape(depth, blocks.shape[2])
     gathered_y = lax.all_gather(solved_coupling, "col", axis=0, tiled=True)
     partial = lax.dot_general(
         gathered_b,

time: 146 us -> 116 us (0.79)
  waiting for transfers between devices: 125 us -> 63.1 us
  blocking collectives: 0 us -> 30.8 us
  local copies, waits for them, and re-layouts: 0.01 us -> 1.84 us
    all_gather x1 -> x0, waiting for transfers between devices: 31 us -> none  [shards(): lax.all_gather(blocks, 'row', axis=1, tiled=True)]
    all_to_all x0 -> x1, blocking collectives: none -> 30.8 us  [pass_figure_on(): lax.all_to_all(jnp.tile(w_in, tray), 'row', split_axis=1, concat_axis=1,...]
    all_gather x1, waiting for transfers between devices: 89.4 us -> 58.7 us  [shards(): gathered_y = lax.all_gather(solved_coupling, 'col', axis=0, tiled=True)]
    another operation x0 -> x2, local copies, waits for them, and re-layouts: none -> 1.7 us  [pass_figure_on(): jnp.tile(w_in, tray)]
  transfers between devices with their start and end apart: 3 -> 2, of which waited for: 3 -> 2; matrix products, arithmetic and copies ran while one was open for 0% -> 2% of each run, Pallas kernels for 0% -> 0%
where the time goes in v1:
time: 116 us; the launch traced here: 115 us
  waiting for transfers between devices  63.1 us (54%)
  blocking collectives  30.8 us (27%)
  between operations  13.4 us (12%)
  matrix products  5.07 us (4%)
  local copies, waits for them, and re-layouts  1.84 us (2%)
    all_gather x1, waiting for transfers between devices, shards(): gathered_y = lax.all_gather(solved_coupling, 'col', axis=0, tiled=True)  58.7 us
    all_to_all x1, blocking collectives, pass_figure_on(): lax.all_to_all(jnp.tile(w_in, tray), 'row', split_axis=1, concat_axis=1,...  30.8 us
    dot_general x1, matrix products, shards(): lax.dot_general(gathered_b, gathered_y, (((0,), (0,)), ((), ())), precisi...  5.07 us
    ppermute x1, waiting for transfers between devices, shards(): other = lax.ppermute(partial, 'layer', [(0, 1), (1, 0)])  3.69 us
  transfers between devices with their start and end apart: 2, of which 2 were waited for; matrix products, arithmetic and copies ran while one was open for 2% of the time, Pallas kernels for 0%

profile of v1, /device:TPU:2, one launch (start us, length us, event | category | flops | bytes accessed | tf_op | source)
XLA Modules:
  0.0 115.5 jit_solution(3972535100533874765)
XLA Ops:
  6.5 0.0 all-gather.2.cloned.1.call-start
  6.5 0.7 all-gather.2.cloned.1.call-update
  7.3 1.2 %copy.5 = f32[2,256,128]{2,0,1:T(2,128)S(1)} copy(f32[2,256,128]{2,1,0:T(8,128)} %bitcast.7) | data formatting | bytes 524288 | tf_op jit(solution)/shard_map/tile | solution.py:12
  8.4 0.5 tile.11
  9.0 30.8 %all_to_all.5 = f32[2,2048,128]{2,0,1:T(2,128)S(1)} all-to-all(f32[2,2048,128]{2,0,1:T(2,128)S(1)} %bitcast.6), channel_id=1, replica_groups=mesh['row'=8,'col'=16,'layer'=2] {'row'}, dimensions={1} | all-to-all | bytes 4194304 | tf_op jit(solution)/shard_map/all_to_all | solution.py:12
  39.7 0.1 copy.6
  39.9 58.7 %all-gather.2.cloned.1.call-done = f32[4096,128]{1,0:T(8,128)} async-done(((f32[256,128]{1,0:T(8,128)}), f32[4096,128]{1,0:T(8,128)}) %all-gather.2.cloned.1.call-update) | async-done | bytes 2097168 | tf_op jit(solution)/shard_map/all_gather | solution.py:18
  98.5 0.0 copy-start
  98.5 5.1 %fusion = f32[128,128]{1,0:T(8,128)S(1)} fusion(f32[4096,128]{1,0:T(8,128)S(1)} %bitcast.5, f32[4096,128]{1,0:T(8,128)} %all-gather.2.cloned.1.call-done), kind=kOutput, calls=%fused_computation.1 | convolution fusion | flops 805306368 | bytes 4259840 | tf_op jit(solution)/shard_map/dot_general | solution.py:19
  103.6 0.7 collective-permute-start
  104.3 3.7 %collective-permute-done = f32[128,128]{1,0:T(8,128)S(1)} collective-permute-done((f32[128,128]{1,0:T(8,128)S(1)}, f32[128,128]{1,0:T(8,128)S(1)}, u32[]{:S(2)}, u32[]{:S(2)}) %collective-permute-start) | collective-permute-done | bytes 65568 | tf_op jit(solution)/shard_map/ppermute | solution.py:26
  108.0 0.0 copy-done
  108.0 0.6 add_subtract_fusion
Async XLA Ops:
  6.5 92.0 %all-gather.2.cloned.1.call-start = ((), (), s32[]{:S(2)}) async-start(), calls=%async_computation.1 | async-start | bytes 2228224 | tf_op jit(solution)/shard_map/all_gather | solution.py:18
  98.5 9.4 %copy-start = (f32[128,128]{1,0:T(8,128)S(1)}, f32[128,128]{1,0:T(8,128)}, u32[]{:S(2)}) copy-start(f32[128,128]{1,0:T(8,128)} %param.3) | copy-start | bytes 196612
  103.6 4.4 %collective-permute-start = (f32[128,128]{1,0:T(8,128)S(1)}, f32[128,128]{1,0:T(8,128)S(1)}, u32[]{:S(2)}, u32[]{:S(2)}) collective-permute-start(f32[128,128]{1,0:T(8,128)S(1)} %fusion), channel_id=1, source_target_pairs={{0,1},{1,0},{2,3},{3,2},{4,5},{5,4},{6,7},{7,6},{8,9},{9,8},{10,11... | collective-permute-start | bytes 196616 | tf_op jit(solution)/shard_map/ppermute | solution.py:26
Sparse Core Ops, SparseCore 0:
  9.9 88.5 all-gather.1
